TPU v7x, 128 devices: a whole 4x4x4 slice. The times are simulated.
128 devices in a mesh: row: 4 (over x), col: 8 (over z_lo, y), layer: 4 (over z_hi, core).
Axes of the slice: x: 4, y: 4, z: 4 (z_hi: 2, z_lo: 2; z = z_hi * 2 + z_lo), core: 2. Of those that a mesh axis runs over, the one named last changes fastest.
Arguments:
- a_blocks: float32 [4096, 4096], P('row', ('col', 'layer')), may hold values from -6 to 6
- mask_a: int32 [64, 64], P('row', ('col', 'layer')), may hold values from 0 to 1, as said below
- b_blocks: float32 [4096, 32768], P('row', ('col', 'layer')), may hold values from -0.25 to 0.25
- mask_b: int32 [64, 512], P('row', ('col', 'layer')), may hold values from 0 to 1
Outputs:
- product: float32 [4096, 32768], P('row', ('col', 'layer'))
Inputs may be any that keep to these rules, and one draw needn't show every extreme that they name: Within one device's shard of mask_a (16 block rows by 2 inner block indices) at most 8 blocks are stored; the shard of the first 16 block rows and first 2 inner indices stores exactly 8.
All inputs are finite; a program needn't handle non-finite values.
Results may differ from a plain program's by a relative error of at most 0.00007.
Values sent between devices are 32-bit elements; how exact they have to be, the bound alone decides.
No kernel may reach another device: no remote copies, remote signals or barrier semaphores. Data moves between devices by JAX's collectives and lax.ppermute only.
A program may use at most 128 MiB of HBM per device.

v0:
```python
import jax
import jax.numpy as jnp
from jax import lax
from jax.sharding import PartitionSpec as P

BLOCK = 64


def expand(mask):
    return jnp.repeat(jnp.repeat(mask, BLOCK, axis=0), BLOCK, axis=1).astype(jnp.float32)


def shards(a_blocks, mask_a, b_blocks, mask_b):
    b_masked = b_blocks * expand(mask_b)
    b_whole = lax.all_gather(b_masked, "row", axis=0, tiled=True)
    a_masked = a_blocks * expand(mask_a)
    return jnp.dot(
        lax.all_gather(a_masked, ("col", "layer"), axis=1, tiled=True),
        b_whole,
        precision=lax.Precision.HIGHEST,
        preferred_element_type=jnp.float32,
    )


def solution(mesh):
    placed = (
        P("row", ("col", "layer")),
        P("row", ("col", "layer")),
        P("row", ("col", "layer")),
        P("row", ("col", "layer")),
    )
    return jax.shard_map(
        shards, mesh=mesh, in_specs=placed, out_specs=P("row", ("col", "layer")), check_vma=False
    )
```

profile of v0, /device:TPU:1, one launch (start us, length us, event | category | flops | bytes accessed | tf_op | source)
XLA Modules:
  0.0 392.4 jit_solution(702926884030204920)
XLA Ops:
  6.5 0.0 copy-start
  6.5 0.0 copy-start.1
  6.5 0.0 all-gather.5.cloned.1.call-start
  6.5 5.4 %copy.8 = f32[1024,1024]{0,1:T(8,128)} copy(f32[1024,1024]{1,0:T(8,128)} %param.6) | data formatting | bytes 8388608 | tf_op args[2]
  11.9 0.7 convert_element_type.25
  12.6 0.1 copy.7
  12.7 0.1 broadcast_in_dim.14
  12.8 0.1 convert_element_type.26
  12.9 5.1 %bitcast_multiply_fusion = f32[1024,1024]{0,1:T(8,128)} fusion(f32[1024,1024]{0,1:T(8,128)} %copy.8, f32[1024,16]{0,1:T(8,128)S(1)} %convert_element_type.26), kind=kLoop, calls=%fused_computation | loop fusion | flops 1048576 | bytes 8454144 | tf_op jit(solution)/shard_map/mul | solution.py:14
  18.0 0.0 all-gather.5.cloned.1.call-update
  18.0 0.0 all-gather.3.cloned.1.call-start
  18.0 0.0 copy-done
  18.1 0.2 copy.6
  18.3 0.0 copy-done.1
  18.3 0.1 broadcast_in_dim.12
  18.4 0.1 convert_element_type.23
  18.4 0.9 bitcast_multiply_fusion.1
  19.3 0.0 all-gather.3.cloned.1.call-update
  19.3 156.1 %all-gather.5.cloned.1.call-done = f32[4096,1024]{0,1:T(8,128)} async-done(((f32[1024,1024]{0,1:T(8,128)}), f32[4096,1024]{0,1:T(8,128)}) %all-gather.5.cloned.1.call-update) | async-done | bytes 16777232 | tf_op jit(solution)/shard_map/all_gather | solution.py:15
  175.4 100.4 %all-gather.3.cloned.1.call-done = f32[1024,4096]{0,1:T(8,128)} async-done(((f32[1024,128]{0,1:T(8,128)}), f32[1024,4096]{0,1:T(8,128)}) %all-gather.3.cloned.1.call-update) | async-done | bytes 16777232 | tf_op jit(solution)/shard_map/all_gather | solution.py:18
  275.8 109.8 %fusion = f32[1024,1024]{1,0:T(8,128)} fusion(f32[1024,4096]{0,1:T(8,128)} %all-gather.3.cloned.1.call-done, f32[4096,1024]{0,1:T(8,128)} %all-gather.5.cloned.1.call-done), kind=kOutput, calls=%fused_computation.2 | convolution fusion | flops 51539607552 | bytes 37748736 | tf_op jit(solution)/shard_map/dot_general | solution.py:17
  (1 shorter events, 0.0 us)
Async XLA Ops:
  6.5 11.5 %copy-start = (f32[1024,128]{1,0:T(8,128)S(1)}, f32[1024,128]{1,0:T(8,128)}, u32[]{:S(2)}) copy-start(f32[1024,128]{1,0:T(8,128)} %param.4) | copy-start | bytes 1572868
  6.5 11.7 %copy-start.1 = (s32[16,2]{0,1:T(2,128)S(1)}, s32[16,2]{0,1:T(2,128)}, u32[]{:S(2)}) copy-start(s32[16,2]{0,1:T(2,128)} %param.5) | copy-start | bytes 388
  6.5 168.9 %all-gather.5.cloned.1.call-start = ((), (), s32[]{:S(2)}) async-start(), calls=%async_computation.1 | async-start | bytes 20971520 | tf_op jit(solution)/shard_map/all_gather | solution.py:15
  18.0 257.8 %all-gather.3.cloned.1.call-start = ((), (), s32[]{:S(2)}) async-start(), calls=%async_computation | async-start | bytes 17301504 | tf_op jit(solution)/shard_map/all_gather | solution.py:18
Sparse Core Ops, SparseCore 0:
  18.1 157.2 all-gather.4
  177.1 98.6 all-gather.2
where the time goes:
time: 393 us; the launch traced here: 392 us
  waiting for transfers between devices  256 us (65%)
  matrix products  110 us (28%)
  between operations  13.4 us (3%)
  other arithmetic  6.62 us (2%)
  local copies, waits for them, and re-layouts  6.02 us (2%)
    all_gather x1, waiting for transfers between devices, shards(): b_whole = lax.all_gather(b_masked, 'row', axis=0, tiled=True)  156 us
    dot_general x1, matrix products, shards(): jnp.dot(lax.all_gather(a_masked, ('col', 'layer'), axis=1, tiled=True), b...  110 us
    all_gather x1, waiting for transfers between devices, shards(): lax.all_gather(a_masked, ('col', 'layer'), axis=1, tiled=True)  100 us
  transfers between devices with their start and end apart: 2, of which 2 were waited for; matrix products, arithmetic and copies ran while one was open for 0% of the time, Pallas kernels for 0%

commit v1 on v0

--- a/solution.py
+++ b/solution.py
@@ -6,13 +6,31 @@
 BLOCK = 64
 
 
+def ring_gather(array, axis, dim):
+    ways, here, turn = (lax.axis_size(axis), lax.axis_index(axis), array.shape[dim])
+    dims = [n * ways if d == dim else n for d, n in enumerate(array.shape)]
+    full = lax.dynamic_update_slice_in_dim(
+        jnp.zeros(dims, array.dtype), array, here * turn, axis=dim
+    )
+    going_up = going_down = array
+    for far in range(1, ways // 2 + 1):
+        going_up = lax.ppermute(going_up, axis, [(d, (d + 1) % ways) for d in range(ways)])
+        full = lax.dynamic_update_slice_in_dim(full, going_up, (here - far) % ways * turn, axis=dim)
+        if 2 * far < ways:
+            going_down = lax.ppermute(going_down, axis, [(d, (d - 1) % ways) for d in range(ways)])
+            full = lax.dynamic_update_slice_in_dim(
+                full, going_down, (here + far) % ways * turn, axis=dim
+            )
+    return full
+
+
 def expand(mask):
     return jnp.repeat(jnp.repeat(mask, BLOCK, axis=0), BLOCK, axis=1).astype(jnp.float32)
 
 
 def shards(a_blocks, mask_a, b_blocks, mask_b):
     b_masked = b_blocks * expand(mask_b)
-    b_whole = lax.all_gather(b_masked, "row", axis=0, tiled=True)
+    b_whole = ring_gather(b_masked, "row", 0)
     a_masked = a_blocks * expand(mask_a)
     return jnp.dot(
         lax.all_gather(a_masked, ("col", "layer"), axis=1, tiled=True),

time: 393 us -> 337 us (0.86)
  waiting for transfers between devices: 256 us -> 172 us
  local copies, waits for them, and re-layouts: 6.02 us -> 29.1 us
    ppermute x0 -> x3, waiting for transfers between devices: none -> 172 us  [the longest x2 172 us: ring_gather(): lax.ppermute(going_up, axis, [(d, (d + 1) % ways) for d in range(ways)])]
    all_gather x1 -> x0, waiting for transfers between devices: 156 us -> none  [shards(): b_whole = lax.all_gather(b_masked, 'row', axis=0, tiled=True)]
    all_gather x1, waiting for transfers between devices: 100 us -> 0.01 us  [shards(): lax.all_gather(a_masked, ('col', 'layer'), axis=1, tiled=True)]
    dynamic_update_slice x0 -> x3, local copies, waits for them, and re-layouts: none -> 14.1 us  [the longest x2 9.44 us: ring_gather(): lax.dynamic_update_slice_in_dim(full, going_up, (here - far) % ways * tur...]
    broadcast_in_dim x0 -> x1, local copies, waits for them, and re-layouts: none -> 8 us  [ring_gather(): jnp.zeros(dims, array.dtype)]
    mul x1 -> x0, other arithmetic: 5.06 us -> none  [shards(): b_masked = b_blocks * expand(mask_b)]
    dynamic_update_slice x0 -> x1, other arithmetic: none -> 4.36 us  [ring_gather(): lax.dynamic_update_slice_in_dim(jnp.zeros(dims, array.dtype), array, here...]
  transfers between devices with their start and end apart: 2 -> 4, of which waited for: 2 -> 2; matrix products, arithmetic and copies ran while one was open for 0% -> 10% of each run, Pallas kernels for 0% -> 0%
where the time goes in v1:
time: 337 us; the launch traced here: 335 us
  waiting for transfers between devices  172 us (51%)
  matrix products  110 us (33%)
  local copies, waits for them, and re-layouts  29.1 us (9%)
  between operations  13.4 us (4%)
  other arithmetic  6.59 us (2%)
  starting transfers between devices  3.6 us (1%)
    ppermute x2, waiting for transfers between devices, ring_gather(): lax.ppermute(going_up, axis, [(d, (d + 1) % ways) for d in range(ways)])  172 us
    dot_general x1, matrix products, shards(): jnp.dot(lax.all_gather(a_masked, ('col', 'layer'), axis=1, tiled=True), b...  110 us
    dynamic_update_slice x2, local copies, waits for them, and re-layouts, ring_gather(): lax.dynamic_update_slice_in_dim(full, going_up, (here - far) % ways * tur...  9.44 us
    broadcast_in_dim x1, local copies, waits for them, and re-layouts, ring_gather(): jnp.zeros(dims, array.dtype)  8 us
  transfers between devices with their start and end apart: 4, of which 2 were waited for; matrix products, arithmetic and copies ran while one was open for 10% of the time, Pallas kernels for 0%

profile of v1, /device:TPU:1, one launch (start us, length us, event | category | flops | bytes accessed | tf_op | source)
XLA Modules:
  0.0 335.0 jit_solution(9454907571476307550)
XLA Ops:
  6.5 0.0 all-gather.2.cloned.1.call-start
  6.5 1.2 copy.6
  7.8 0.7 convert_element_type.22
  8.5 0.1 broadcast_in_dim.15
  8.5 0.1 convert_element_type.23
  8.6 0.9 bitcast_multiply_fusion.1
  9.5 0.0 all-gather.2.cloned.1.call-update
  9.5 5.3 %copy.8 = f32[1024,1024]{0,1:T(8,128)} copy(f32[1024,1024]{1,0:T(8,128)} %param.6) | data formatting | bytes 8388608 | tf_op args[2]
  14.9 0.7 convert_element_type.25
  15.5 0.1 copy.7
  15.6 0.1 broadcast_in_dim.18
  15.7 0.1 convert_element_type.26
  15.8 0.0 copy-start
  15.8 8.0 %broadcast_in_dim.17 = f32[4096,1024]{0,1:T(8,128)} broadcast(f32[]{:T(128)} %constant.30.clone.1), dimensions={} | broadcast | bytes 16777220 | tf_op jit(solution)/shard_map/broadcast_in_dim | solution.py:13
  23.8 0.0 copy-done
  23.8 4.4 %constant_dynamic-update-slice_fusion.3 = (f32[4096,1024]{0,1:T(8,128)}, f32[1024,1024]{0,1:T(8,128)}) fusion(f32[4096,1024]{0,1:T(8,128)} %broadcast_in_dim.17, s32[]{:T(128)S(6)} %select_n.27, f32[1024,1024]{0,1:T(8,128)S(1)} %copy-done, f32[1024,16]{0,1:T(8,128)S(1)} %convert_element_type.26), kind=kLoop, calls=%fused_computation.5 | loop fusion | flops 1048576 | bytes 12648452 | tf_op jit(solution)/shard_map/dynamic_update_slice | solution.py:12
  28.2 2.0 collective-permute-start
  30.2 1.3 collective-permute-start.1
  31.5 90.2 %collective-permute-done = f32[1024,1024]{0,1:T(8,128)} collective-permute-done((f32[1024,1024]{0,1:T(8,128)}, f32[1024,1024]{0,1:T(8,128)}, u32[]{:S(2)}, u32[]{:S(2)}) %collective-permute-start) | collective-permute-done | bytes 4194336 | tf_op jit(solution)/shard_map/ppermute | solution.py:17
  121.7 0.2 collective-permute-start.2
  122.0 4.8 %constant_dynamic-update-slice_fusion.2 = f32[4096,1024]{0,1:T(8,128)} fusion(f32[4096,1024]{0,1:T(8,128)} %get-tuple-element.5, f32[1024,1024]{0,1:T(8,128)} %collective-permute-done, s32[]{:T(128)S(6)} %select_n.29), kind=kLoop, calls=%fused_computation.4 | loop fusion | bytes 8388612 | tf_op jit(solution)/shard_map/dynamic_update_slice | solution.py:18
  126.7 0.0 collective-permute-done.1
  126.7 4.7 %constant_dynamic-update-slice_fusion.1 = f32[4096,1024]{0,1:T(8,128)} fusion(f32[4096,1024]{0,1:T(8,128)} %constant_dynamic-update-slice_fusion.2, f32[1024,1024]{0,1:T(8,128)} %collective-permute-done.1, s32[]{:T(128)S(6)} %select_n.31), kind=kLoop, calls=%fused_computation.3 | loop fusion | bytes 8388612 | tf_op jit(solution)/shard_map/dynamic_update_slice | solution.py:21
  131.4 82.3 %collective-permute-done.2 = f32[1024,1024]{0,1:T(8,128)} collective-permute-done((f32[1024,1024]{0,1:T(8,128)}, f32[1024,1024]{0,1:T(8,128)}, u32[]{:S(2)}, u32[]{:S(2)}) %collective-permute-start.2) | collective-permute-done | bytes 4194336 | tf_op jit(solution)/shard_map/ppermute | solution.py:17
  213.7 4.7 %constant_dynamic-update-slice_fusion = f32[4096,1024]{0,1:T(8,128)} fusion(f32[4096,1024]{0,1:T(8,128)} %constant_dynamic-update-slice_fusion.1, f32[1024,1024]{0,1:T(8,128)} %collective-permute-done.2, s32[]{:T(128)S(6)} %select_n.33), kind=kLoop, calls=%fused_computation.2 | loop fusion | bytes 8388612 | tf_op jit(solution)/shard_map/dynamic_update_slice | solution.py:18
  218.4 0.0 all-gather.2.cloned.1.call-done
  218.4 109.8 %fusion = f32[1024,1024]{1,0:T(8,128)} fusion(f32[1024,4096]{0,1:T(8,128)} %all-gather.2.cloned.1.call-done, f32[4096,1024]{0,1:T(8,128)} %constant_dynamic-update-slice_fusion), kind=kOutput, calls=%fused_computation.6 | convolution fusion | flops 51539607552 | bytes 37748736 | tf_op jit(solution)/shard_map/dot_general | solution.py:35
Async XLA Ops:
  6.5 211.9 %all-gather.2.cloned.1.call-start = ((), (), s32[]{:S(2)}) async-start(), calls=%async_computation | async-start | bytes 17301504 | tf_op jit(solution)/shard_map/all_gather | solution.py:36
  15.8 8.0 %copy-start = (f32[1024,1024]{0,1:T(8,128)S(1)}, f32[1024,1024]{0,1:T(8,128)}, u32[]{:S(2)}) copy-start(f32[1024,1024]{0,1:T(8,128)} %copy.8) | copy-start | bytes 12582916
  28.2 93.5 %collective-permute-start = (f32[1024,1024]{0,1:T(8,128)}, f32[1024,1024]{0,1:T(8,128)}, u32[]{:S(2)}, u32[]{:S(2)}) collective-permute-start(f32[1024,1024]{0,1:T(8,128)} %get-tuple-element.6), channel_id=1, source_target_pairs={{0,32},{32,64},{64,96},{96,0},{1,33},{33,65},{65,97},{97,1},{2,34}... | collective-permute-start | bytes 12582920 | tf_op jit(solution)/shard_map/ppermute | solution.py:17
  30.2 96.5 %collective-permute-start.1 = (f32[1024,1024]{0,1:T(8,128)}, f32[1024,1024]{0,1:T(8,128)}, u32[]{:S(2)}, u32[]{:S(2)}) collective-permute-start(f32[1024,1024]{0,1:T(8,128)} %get-tuple-element.6), channel_id=1, source_target_pairs={{0,96},{32,0},{64,32},{96,64},{1,97},{33,1},{65,33},{97,65},{2,98}... | collective-permute-start | bytes 12582920 | tf_op jit(solution)/shard_map/ppermute | solution.py:20
  121.7 92.0 %collective-permute-start.2 = (f32[1024,1024]{0,1:T(8,128)}, f32[1024,1024]{0,1:T(8,128)}, u32[]{:S(2)}, u32[]{:S(2)}) collective-permute-start(f32[1024,1024]{0,1:T(8,128)} %collective-permute-done), channel_id=1, source_target_pairs={{0,32},{32,64},{64,96},{96,0},{1,33},{33,65},{65,97},{97,1},{2,34}... | collective-permute-start | bytes 12582920 | tf_op jit(solution)/shard_map/ppermute | solution.py:17
Sparse Core Ops, SparseCore 0:
  9.6 100.8 all-gather.1
